TPU v7x, 32 devices: a whole 2x2x4 slice. The times are simulated.
32 devices in a mesh: scen: 2 (over y), site: 4 (over z), sub: 2 (over x), var: 2 (over core).
Axes of the slice: x: 2, y: 2, z: 4, core: 2. Of those that a mesh axis runs over, the one named last changes fastest.
Arguments:
- green_tensor: bfloat16 [8, 2, 16, 2, 2, 3, 32, 6, 128], P(('scen', 'site'), 'sub', None, 'var'), parts along dimension 0, may hold values from -0.078125 to 0.078125
- rupture_spectra: bfloat16 [2, 2, 512, 6, 1024], P(None, None, ('scen', 'var'), None, ('sub', 'site')), parts along dimension 2, may hold values from -6 to 6
- pair_site: int32 [8, 2, 16], P(('scen', 'site'), 'sub'), parts along dimension 0, may hold values from 0 to 3, as said below
- pair_block: int32 [8, 2, 16], P(('scen', 'site'), 'sub'), parts along dimension 0, may hold values from 0 to 3, as said below
- pair_count: int32 [8, 2, 16], P(('scen', 'site'), 'sub'), parts along dimension 0, may hold values from 0 to 128, as said below
- band_offset: int32 [2], P('scen'), parts along dimension 0, may hold values from 0 to 127
Outputs:
- site_spectra: float32 [2, 2, 3, 256, 1024], P(None, None, None, 'var', ('scen', 'site', 'sub')), parts along dimension 4
There are 2 independent parts, one for each index of `scen`. A program takes and returns all parts, laid end to end along the dimension named above; each array names one. Nothing has to cross between parts.
Inputs may be any that keep to these rules, and one draw needn't show every extreme that they name: On each device the live slots come first and are followed by unused slots; live slots name distinct pairs; unused slots have pair_count 0. No device has more than 12 live slots, and some device of every draw has exactly 12. `pair_site`: site block within the device's 4 site blocks. `pair_block`: subfault block within the device's group of 4 blocks.
All inputs are finite; a program needn't handle non-finite values.
Results may differ from a plain program's by a relative error of at most 0.0003.
Values may be sent and summed in bfloat16 or wider, within the bound.
No kernel may reach another device: no remote copies, remote signals or barrier semaphores. Data moves between devices by JAX's collectives and lax.ppermute only.
A program may use at most 64 MiB of HBM per device.

v0:
```python
import jax
import jax.numpy as jnp
from jax import lax
from jax.sharding import PartitionSpec as P

FREQS = 2
SITE_BLOCKS = 4
CORNER = 48.0


def pair_terms(
    totals,
    tiles,
    spectra,
    spec_start,
    total_start,
    site_table,
    block_table,
    count_table,
    slot_count,
):
    width = tiles.shape[1]
    block_sites = tiles.shape[4]
    variants = spectra.shape[2]
    columns = jnp.arange(128, dtype=jnp.int32)

    def add_pair(slot, totals):
        tensor_tile = lax.dynamic_index_in_dim(tiles, slot, 0, keepdims=False)
        spectrum = lax.dynamic_slice(
            spectra, (spec_start, 0, 0, 0, block_table[slot] * 128), (width, 2, variants, 6, 128)
        )
        keep_mask = (columns < count_table[slot]).astype(spectrum.dtype)
        spectrum = spectrum * keep_mask
        products = jnp.einsum(
            "fpcsmk,fqvmk->fpqcvs", tensor_tile, spectrum, preferred_element_type=jnp.float32
        )
        real_part = products[:, 0, 0] - products[:, 1, 1]
        imag_part = products[:, 0, 1] + products[:, 1, 0]
        contrib = jnp.stack([real_part, imag_part], axis=1)
        corner = (total_start, 0, 0, 0, site_table[slot] * block_sites)
        current = lax.dynamic_slice(totals, corner, contrib.shape)
        return lax.dynamic_update_slice(totals, current + contrib, corner)

    return lax.fori_loop(0, slot_count, add_pair, totals)


def shards(green_tensor, rupture_spectra, pair_site, pair_block, pair_count, band_offset):
    site_table = pair_site[0, 0]
    block_table = pair_block[0, 0]
    count_table = pair_count[0, 0]
    block_sites = green_tensor.shape[6]
    site_width = SITE_BLOCKS * block_sites
    spectra = lax.all_gather(rupture_spectra, "site", axis=4, tiled=True)
    slot_count = green_tensor.shape[2]
    local_vars = spectra.shape[2]
    empty = jnp.zeros((FREQS, 2, 3, local_vars, site_width), jnp.float32)
    piece_start = jnp.int32(0)
    totals = pair_terms(
        empty,
        lax.all_gather(green_tensor, "var", axis=3, tiled=True)[0, 0],
        spectra,
        piece_start,
        piece_start,
        site_table,
        block_table,
        count_table,
        slot_count,
    )
    partial_value = lax.psum_scatter(totals, "sub", scatter_dimension=4, tiled=True)
    freq_index = (band_offset[0] + jnp.arange(FREQS, dtype=jnp.int32)).astype(jnp.float32)
    brune = 1.0 / (1.0 + (freq_index / CORNER) ** 2)
    return partial_value * brune[:, None, None, None, None]


def solution(mesh):
    return jax.shard_map(
        shards,
        mesh=mesh,
        in_specs=(
            P(("scen", "site"), "sub", None, "var", None, None, None, None, None),
            P(None, None, ("scen", "var"), None, ("sub", "site")),
            P(("scen", "site"), "sub", None),
            P(("scen", "site"), "sub", None),
            P(("scen", "site"), "sub", None),
            P("scen"),
        ),
        out_specs=P(None, None, None, "var", ("scen", "site", "sub")),
        check_vma=False,
    )
```

profile of v0, /device:TPU:0, one launch (start us, length us, event | category | flops | bytes accessed | tf_op | source)
XLA Modules:
  0.0 213.4 jit_solution(682382720835881932)
XLA Ops:
  6.5 0.7 all-gather.3.cloned.1.call-update
  7.3 0.7 all-gather.5.cloned.1.call-update
  8.1 67.0 %all-gather.3.cloned.1.call-done = bf16[2,2,128,6,512]{4,2,3,1,0:T(8,128)(2,1)} async-done(((bf16[2,2,128,6,128]{4,2,3,1,0:T(8,128)(2,1)}), bf16[2,2,128,6,512]{4,2,3,1,0:T(8,128)(2,1)}) %all-gather.3.cloned.1.call-update) | async-done | bytes 3145744 | tf_op jit(solution)/shard_map/all_gather | solution.py:53
  75.1 21.5 %all-gather.5.cloned.1.call-done = bf16[1,1,16,2,2,3,32,6,128]{8,6,7,5,4,3,2,1,0:T(8,128)(2,1)} async-done(((bf16[1,1,16,1,2,3,32,6,128]{8,6,7,5,4,3,2,1,0:T(8,128)(2,1)}), bf16[1,1,16,2,2,3,32,6,128]{8,6,7,5,4,3,2,1,0:T(8,128)(2,1)}) %all-gather.5.cloned.1.call-update) | async-done | bytes 9437200 | tf_op jit(solution)/shard_map/all_gather | solution.py:60
  96.7 88.6 %while.14 = (s32[]{:T(128)}, f32[2,2,3,128,128]{3,4,2,1,0:T(8,128)S(1)}, s32[16]{0:T(128)S(1)}, s32[16]{0:T(128)S(1)}, bf16[2,2,128,6,512]{4,2,3,1,0:T(8,128)(2,...) while((s32[]{:T(128)}, ...), condition=%wide.region_1.2_spmd.clone, body=%wide.region_0.1_spmd.clone.sunk | while | flops 152715536 | bytes 3343629 | solution.py:44
  99.2 1.7 convolution_bitcast_fusion.2
  104.7 1.7 convolution_bitcast_fusion.2
  110.2 1.7 convolution_bitcast_fusion.2
  115.8 1.7 convolution_bitcast_fusion.2
  121.3 1.7 convolution_bitcast_fusion.2
  126.9 1.7 convolution_bitcast_fusion.2
  132.4 1.7 convolution_bitcast_fusion.2
  137.9 1.7 convolution_bitcast_fusion.2
  143.5 1.7 convolution_bitcast_fusion.2
  149.0 1.7 convolution_bitcast_fusion.2
  154.6 1.7 convolution_bitcast_fusion.2
  160.1 1.7 convolution_bitcast_fusion.2
  165.6 1.7 convolution_bitcast_fusion.2
  171.2 1.7 convolution_bitcast_fusion.2
  176.7 1.7 convolution_bitcast_fusion.2
  182.2 1.7 convolution_bitcast_fusion.2
  185.4 0.9 copy-done
  186.9 18.1 %reduce-scatter.2.cloned.1.call-done = f32[2,2,3,128,64]{3,4,2,1,0:T(8,128)} async-done(((f32[2,2,3,128,128]{3,4,2,1,0:T(8,128)}), f32[2,2,3,128,64]{3,4,2,1,0:T(8,128)}) %reduce-scatter.2.cloned.1.call-update) | async-done | bytes 393232 | tf_op jit(solution)/shard_map/reduce_scatter | solution.py:69
  205.0 1.8 broadcast_multiply_fusion
  (141 shorter events, 40.0 us)
Async XLA Ops:
  6.5 90.2 %copy-start.1 = (s32[1,1,16]{2,1,0:T(1,128)S(1)}, s32[1,1,16]{2,1,0:T(1,128)}, u32[]{:S(2)}) copy-start(s32[1,1,16]{2,1,0:T(1,128)} %param.10) | copy-start | bytes 196
  6.5 90.2 %copy-start.2 = (s32[1,1,16]{2,1,0:T(1,128)S(1)}, s32[1,1,16]{2,1,0:T(1,128)}, u32[]{:S(2)}) copy-start(s32[1,1,16]{2,1,0:T(1,128)} %param.11) | copy-start | bytes 196
  6.5 90.2 %copy-start.3 = (s32[1,1,16]{2,1,0:T(1,128)S(1)}, s32[1,1,16]{2,1,0:T(1,128)}, u32[]{:S(2)}) copy-start(s32[1,1,16]{2,1,0:T(1,128)} %param.12) | copy-start | bytes 196
  6.5 68.5 %all-gather.3.cloned.1.call-start = ((), (), s32[]{:S(2)}) async-start(), calls=%async_computation.1 | async-start | bytes 3932160 | tf_op jit(solution)/shard_map/all_gather | solution.py:53
  7.3 89.4 %all-gather.5.cloned.1.call-start = ((), (), s32[]{:S(2)}) async-start(), calls=%async_computation.2 | async-start | bytes 14155776 | tf_op jit(solution)/shard_map/all_gather | solution.py:60
  8.0 197.0 %reduce-scatter.2.cloned.1.call-start = ((), (), s32[]{:S(2)}) async-start(), calls=%async_computation.3 | async-start | bytes 1179648 | tf_op jit(solution)/shard_map/reduce_scatter | solution.py:69
  185.3 0.9 copy-start
Sparse Core Ops, SparseCore 0:
  8.9 66.1 all-gather.2
  76.6 19.9 all-gather.4
  186.4 18.5 reduce-scatter.1
where the time goes:
time: 214 us; the launch traced here: 213 us
  waiting for transfers between devices  108 us (50%)
  local copies, waits for them, and re-layouts  29.8 us (14%)
  matrix products  27.9 us (13%)
  loops' own time  20.9 us (10%)
  between operations  13.8 us (6%)
  other arithmetic  12.8 us (6%)
    all_gather x1, waiting for transfers between devices, shards(): spectra = lax.all_gather(rupture_spectra, 'site', axis=4, tiled=True)  67 us
    dot_general x16, matrix products, add_pair(): jnp.einsum('fpcsmk,fqvmk->fpqcvs', tensor_tile, spectrum, preferred_eleme...  27.9 us
    all_gather x1, waiting for transfers between devices, shards(): lax.all_gather(green_tensor, 'var', axis=3, tiled=True)[0, 0]  21.5 us
    another operation x1, loops' own time, pair_terms(): return lax.fori_loop(0, slot_count, add_pair, totals)  20.9 us
    reduce_scatter x1, waiting for transfers between devices, shards(): lax.psum_scatter(totals, 'sub', scatter_dimension=4, tiled=True)  18.1 us
    convert_element_type x16, other arithmetic, add_pair(): keep_mask = (columns < count_table[slot]).astype(spectrum.dtype)  9.88 us
    dynamic_slice x16, local copies, waits for them, and re-layouts, add_pair(): keep_mask = (columns < count_table[slot]).astype(spectrum.dtype)  9.52 us
    dynamic_slice x16, local copies, waits for them, and re-layouts, add_pair(): corner = (total_start, 0, 0, 0, site_table[slot] * block_sites)  9.52 us
  transfers between devices with their start and end apart: 3, of which 3 were waited for; matrix products, arithmetic and copies ran while one was open for 0% of the time, Pallas kernels for 0%

commit v1 on v0

--- a/solution.py
+++ b/solution.py
@@ -6,6 +6,24 @@
 FREQS = 2
 SITE_BLOCKS = 4
 CORNER = 48.0
+
+
+def collect(array, axis, dim):
+    ways, here, step = (lax.axis_size(axis), lax.axis_index(axis), array.shape[dim])
+    lengths = [n * ways if d == dim else n for d, n in enumerate(array.shape)]
+    full = lax.dynamic_update_slice_in_dim(
+        jnp.zeros(lengths, array.dtype), array, here * step, axis=dim
+    )
+    going_up = going_down = array
+    for far in range(1, ways // 2 + 1):
+        going_up = lax.ppermute(going_up, axis, [(d, (d + 1) % ways) for d in range(ways)])
+        full = lax.dynamic_update_slice_in_dim(full, going_up, (here - far) % ways * step, axis=dim)
+        if 2 * far < ways:
+            going_down = lax.ppermute(going_down, axis, [(d, (d - 1) % ways) for d in range(ways)])
+            full = lax.dynamic_update_slice_in_dim(
+                full, going_down, (here + far) % ways * step, axis=dim
+            )
+    return full
 
 
 def pair_terms(
@@ -50,7 +68,7 @@
     count_table = pair_count[0, 0]
     block_sites = green_tensor.shape[6]
     site_width = SITE_BLOCKS * block_sites
-    spectra = lax.all_gather(rupture_spectra, "site", axis=4, tiled=True)
+    spectra = collect(rupture_spectra, "site", 4)
     slot_count = green_tensor.shape[2]
     local_vars = spectra.shape[2]
     empty = jnp.zeros((FREQS, 2, 3, local_vars, site_width), jnp.float32)

time: 214 us -> 183 us (0.86)
  waiting for transfers between devices: 108 us -> 63.3 us
  local copies, waits for them, and re-layouts: 29.8 us -> 37.2 us
  starting transfers between devices: 0.08 us -> 5.09 us
    all_gather x1 -> x0, waiting for transfers between devices: 67 us -> none  [shards(): spectra = lax.all_gather(rupture_spectra, 'site', axis=4, tiled=True)]
    ppermute x0 -> x3, waiting for transfers between devices: none -> 46.3 us  [the longest x2 34.6 us: collect(): lax.ppermute(going_up, axis, [(d, (d + 1) % ways) for d in range(ways)])]
    all_gather x1, waiting for transfers between devices: 21.5 us -> 0.01 us  [shards(): lax.all_gather(green_tensor, 'var', axis=3, tiled=True)[0, 0]]
    ppermute x0 -> x3, starting transfers between devices: none -> 5.05 us  [the longest x2 3.03 us: collect(): lax.ppermute(going_up, axis, [(d, (d + 1) % ways) for d in range(ways)])]
    dynamic_update_slice x0 -> x4, local copies, waits for them, and re-layouts: none -> 4.04 us  [the longest x2 2.02 us: collect(): lax.dynamic_update_slice_in_dim(full, going_up, (here - far) % ways * ste...]
  transfers between devices with their start and end apart: 3 -> 5, of which waited for: 3 -> 4; matrix products, arithmetic and copies ran while one was open for 0% -> 3% of each run, Pallas kernels for 0% -> 0%
where the time goes in v1:
time: 183 us; the launch traced here: 182 us
  waiting for transfers between devices  63.3 us (35%)
  local copies, waits for them, and re-layouts  37.2 us (20%)
  matrix products  27.8 us (15%)
  loops' own time  21.5 us (12%)
  between operations  14.1 us (8%)
  other arithmetic  13.1 us (7%)
  starting transfers between devices  5.09 us (3%)
    ppermute x2, waiting for transfers between devices, collect(): lax.ppermute(going_up, axis, [(d, (d + 1) % ways) for d in range(ways)])  34.6 us
    dot_general x16, matrix products, add_pair(): jnp.einsum('fpcsmk,fqvmk->fpqcvs', tensor_tile, spectrum, preferred_eleme...  27.8 us
    another operation x1, loops' own time, pair_terms(): return lax.fori_loop(0, slot_count, add_pair, totals)  21.5 us
    reduce_scatter x1, waiting for transfers between devices, shards(): lax.psum_scatter(totals, 'sub', scatter_dimension=4, tiled=True)  16.3 us
    ppermute x1, waiting for transfers between devices, collect(): lax.ppermute(going_down, axis, [(d, (d - 1) % ways) for d in range(ways)])  11.7 us
    convert_element_type x16, other arithmetic, add_pair(): keep_mask = (columns < count_table[slot]).astype(spectrum.dtype)  10.2 us
    dynamic_slice x16, local copies, waits for them, and re-layouts, add_pair(): keep_mask = (columns < count_table[slot]).astype(spectrum.dtype)  9.84 us
    dynamic_slice x16, local copies, waits for them, and re-layouts, add_pair(): corner = (total_start, 0, 0, 0, site_table[slot] * block_sites)  9.84 us
  transfers between devices with their start and end apart: 5, of which 4 were waited for; matrix products, arithmetic and copies ran while one was open for 3% of the time, Pallas kernels for 0%

profile of v1, /device:TPU:0, one launch (start us, length us, event | category | flops | bytes accessed | tf_op | source)
XLA Modules:
  0.0 182.1 jit_solution(3191286904196241499)
XLA Ops:
  7.7 3.0 %collective-permute-start = (bf16[2,2,128,6,128]{4,2,3,1,0:T(8,128)(2,1)S(1)}, bf16[2,2,128,6,128]{4,2,3,1,0:T(8,128)(2,1)S(1)}, u32[]{:S(2)}, u32[]{:S(2)}) collective-permute-start(bf16[2,2,128,6,128]{4,2,3,1,0:T(8,128)(2,1)S(1)} %copy-done.1), channel_id=1, source_target_pairs={{0,4},{4,8},{8,12},{12,0},{1,5},{5,9},{9,13},{13,1},{2,6},{6,10},{... | collective-permute-start | bytes 2359304 | tf_op jit(solution)/shard_map/ppermute | solution.py:19
  10.7 2.0 %collective-permute-start.1 = (bf16[2,2,128,6,128]{4,2,3,1,0:T(8,128)(2,1)S(1)}, bf16[2,2,128,6,128]{4,2,3,1,0:T(8,128)(2,1)S(1)}, u32[]{:S(2)}, u32[]{:S(2)}) collective-permute-start(bf16[2,2,128,6,128]{4,2,3,1,0:T(8,128)(2,1)S(1)} %copy-done.1), channel_id=1, source_target_pairs={{0,12},{4,0},{8,4},{12,8},{1,13},{5,1},{9,5},{13,9},{2,14},{6,2},{... | collective-permute-start | bytes 2359304 | tf_op jit(solution)/shard_map/ppermute | solution.py:22
  12.7 18.4 %collective-permute-done = bf16[2,2,128,6,128]{4,2,3,1,0:T(8,128)(2,1)S(1)} collective-permute-done((bf16[2,2,128,6,128]{4,2,3,1,0:T(8,128)(2,1)S(1)}, bf16[2,2,128,6,128]{4,2,3,1,0:T(8,128)(2,1)S(1)}, u32[]{:S(2)}, u32[]{:S(2)}) %collective-permute-start) | collective-permute-done | bytes 786464 | tf_op jit(solution)/shard_map/ppermute | solution.py:19
  31.1 2.0 %broadcast_in_dim.11 = bf16[2,2,128,6,512]{4,2,3,1,0:T(8,128)(2,1)} broadcast(bf16[]{:T(256)} %constant.82.clone.1), dimensions={} | broadcast | bytes 3145730 | tf_op jit(solution)/shard_map/broadcast_in_dim | solution.py:15
  35.1 11.7 %collective-permute-done.1 = bf16[2,2,128,6,128]{4,2,3,1,0:T(8,128)(2,1)S(1)} collective-permute-done((bf16[2,2,128,6,128]{4,2,3,1,0:T(8,128)(2,1)S(1)}, bf16[2,2,128,6,128]{4,2,3,1,0:T(8,128)(2,1)S(1)}, u32[]{:S(2)}, u32[]{:S(2)}) %collective-permute-start.1) | collective-permute-done | bytes 786464 | tf_op jit(solution)/shard_map/ppermute | solution.py:22
  47.8 16.2 %collective-permute-done.2 = bf16[2,2,128,6,128]{4,2,3,1,0:T(8,128)(2,1)S(1)} collective-permute-done((bf16[2,2,128,6,128]{4,2,3,1,0:T(8,128)(2,1)S(1)}, bf16[2,2,128,6,128]{4,2,3,1,0:T(8,128)(2,1)S(1)}, u32[]{:S(2)}, u32[]{:S(2)}) %collective-permute-start.2) | collective-permute-done | bytes 786464 | tf_op jit(solution)/shard_map/ppermute | solution.py:19
  65.1 90.4 %while.14 = (s32[]{:T(128)}, f32[2,2,3,128,128]{3,4,2,1,0:T(8,128)S(1)}, s32[16]{0:T(128)S(1)}, s32[16]{0:T(128)S(1)}, bf16[2,2,128,6,512]{4,2,3,1,0:T(8,128)(2,...) while((s32[]{:T(128)}, ...), condition=%wide.region_1.2_spmd.clone, body=%wide.region_0.1_spmd.clone.sunk | while | flops 152715536 | bytes 3343629 | solution.py:62
  67.7 1.7 convolution_bitcast_fusion.2
  79.0 1.7 convolution_bitcast_fusion.2
  84.6 1.7 convolution_bitcast_fusion.2
  90.3 1.7 convolution_bitcast_fusion.2
  95.9 1.7 convolution_bitcast_fusion.2
  101.6 1.7 convolution_bitcast_fusion.2
  107.2 1.7 convolution_bitcast_fusion.2
  112.9 1.7 convolution_bitcast_fusion.2
  118.5 1.7 convolution_bitcast_fusion.2
  124.2 1.7 convolution_bitcast_fusion.2
  129.8 1.7 convolution_bitcast_fusion.2
  135.5 1.7 convolution_bitcast_fusion.2
  141.1 1.7 convolution_bitcast_fusion.2
  146.8 1.7 convolution_bitcast_fusion.2
  152.4 1.7 convolution_bitcast_fusion.2
  157.1 16.3 %reduce-scatter.2.cloned.1.call-done = f32[2,2,3,128,64]{3,4,2,1,0:T(8,128)} async-done(((f32[2,2,3,128,128]{3,4,2,1,0:T(8,128)}), f32[2,2,3,128,64]{3,4,2,1,0:T(8,128)}) %reduce-scatter.2.cloned.1.call-update) | async-done | bytes 393232 | tf_op jit(solution)/shard_map/reduce_scatter | solution.py:87
  173.4 1.8 %broadcast_multiply_fusion = f32[2,2,3,128,64]{3,4,2,1,0:T(8,128)} fusion(f32[2,2,3,128,64]{3,4,2,1,0:T(8,128)} %reduce-scatter.2.cloned.1.call-done, f32[2]{0:T(128)S(1)} %add_divide_fusion), kind=kLoop, calls=%fused_computation.19 | loop fusion | flops 98304 | bytes 786440 | tf_op jit(solution)/shard_map/mul | solution.py:90
  (151 shorter events, 48.9 us)
Async XLA Ops:
  6.5 1.1 copy-start.1
  6.5 58.5 %all-gather.2.cloned.1.call-start = ((), (), s32[]{:S(2)}) async-start(), calls=%async_computation.1 | async-start | bytes 14155776 | tf_op jit(solution)/shard_map/all_gather | solution.py:78
  7.3 166.2 %reduce-scatter.2.cloned.1.call-start = ((), (), s32[]{:S(2)}) async-start(), calls=%async_computation.2 | async-start | bytes 1179648 | tf_op jit(solution)/shard_map/reduce_scatter | solution.py:87
  7.7 23.5 %collective-permute-start = (bf16[2,2,128,6,128]{4,2,3,1,0:T(8,128)(2,1)S(1)}, bf16[2,2,128,6,128]{4,2,3,1,0:T(8,128)(2,1)S(1)}, u32[]{:S(2)}, u32[]{:S(2)}) collective-permute-start(bf16[2,2,128,6,128]{4,2,3,1,0:T(8,128)(2,1)S(1)} %copy-done.1), channel_id=1, source_target_pairs={{0,4},{4,8},{8,12},{12,0},{1,5},{5,9},{9,13},{13,1},{2,6},{6,10},{... | collective-permute-start | bytes 2359304 | tf_op jit(solution)/shard_map/ppermute | solution.py:19
  10.7 36.1 %collective-permute-start.1 = (bf16[2,2,128,6,128]{4,2,3,1,0:T(8,128)(2,1)S(1)}, bf16[2,2,128,6,128]{4,2,3,1,0:T(8,128)(2,1)S(1)}, u32[]{:S(2)}, u32[]{:S(2)}) collective-permute-start(bf16[2,2,128,6,128]{4,2,3,1,0:T(8,128)(2,1)S(1)} %copy-done.1), channel_id=1, source_target_pairs={{0,12},{4,0},{8,4},{12,8},{1,13},{5,1},{9,5},{13,9},{2,14},{6,2},{... | collective-permute-start | bytes 2359304 | tf_op jit(solution)/shard_map/ppermute | solution.py:22
  31.1 32.9 %collective-permute-start.2 = (bf16[2,2,128,6,128]{4,2,3,1,0:T(8,128)(2,1)S(1)}, bf16[2,2,128,6,128]{4,2,3,1,0:T(8,128)(2,1)S(1)}, u32[]{:S(2)}, u32[]{:S(2)}) collective-permute-start(bf16[2,2,128,6,128]{4,2,3,1,0:T(8,128)(2,1)S(1)} %collective-permute-done), channel_id=1, source_target_pairs={{0,4},{4,8},{8,12},{12,0},{1,5},{5,9},{9,13},{13,1},{2,6},{6,10},{... | collective-permute-start | bytes 2359304 | tf_op jit(solution)/shard_map/ppermute | solution.py:19
  34.1 31.0 %copy-start.2 = (s32[1,1,16]{2,1,0:T(1,128)S(1)}, s32[1,1,16]{2,1,0:T(1,128)}, u32[]{:S(2)}) copy-start(s32[1,1,16]{2,1,0:T(1,128)} %param.10) | copy-start | bytes 196
  34.1 31.0 %copy-start.3 = (s32[1,1,16]{2,1,0:T(1,128)S(1)}, s32[1,1,16]{2,1,0:T(1,128)}, u32[]{:S(2)}) copy-start(s32[1,1,16]{2,1,0:T(1,128)} %param.11) | copy-start | bytes 196
  34.1 31.0 %copy-start.4 = (s32[1,1,16]{2,1,0:T(1,128)S(1)}, s32[1,1,16]{2,1,0:T(1,128)}, u32[]{:S(2)}) copy-start(s32[1,1,16]{2,1,0:T(1,128)} %param.12) | copy-start | bytes 196
  155.5 0.9 copy-start
Sparse Core Ops, SparseCore 0:
  8.9 24.4 all-gather.1
  156.6 16.7 reduce-scatter.1
